TPU v7x, 128 devices: a whole 4x4x4 slice. The times are simulated.
128 devices in a mesh: box: 64 (over y, z_hi, x, core), dir: 2 (over z_lo).
Axes of the slice: x: 4, y: 4, z: 4 (z_hi: 2, z_lo: 2; z = z_hi * 2 + z_lo), core: 2. Of those that a mesh axis runs over, the one named last changes fastest.
Arguments:
- sources: bfloat16 [256, 2, 32, 256], P('box'), may hold values from -6 to 6
- encode: bfloat16 [2, 1024, 256], P(None, 'dir'), may hold values from -0.375 to 0.375
- kernel: float32 [1024, 2, 16, 128], P(('dir', 'box')), may hold values from -0.25 to 0.25
- decode: bfloat16 [2, 1024, 256], P(None, 'dir'), may hold values from -0.1875 to 0.1875
- near_blocks: bfloat16 [256, 28, 2, 256, 256], P('box', 'dir'), may hold values from -0.078125 to 0.078125
- near_list: int32 [256, 28], P('box', 'dir'), may hold values from 0 to 255, as said below
- near_mask: int32 [256, 28], P('box', 'dir'), may hold values from 0 to 1, as said below
- box_cell: int32 [256], replicated, may hold values from 0 to 255, as said below
Outputs:
- product: float32 [256, 2, 32, 256], P('box', None, None, 'dir')
Inputs may be any that keep to these rules, and one draw needn't show every extreme that they name: A permutation of the cells: box b lies in cell box_cell[b] = (ix * 8 + iy) * 4 + iz of the 8 x 8 x 4 grid. Where near_mask[b, s] is 1, near_list[b, s] is the box whose cell differs from box b's cell by -1, 0 or 1 along each dimension, each such box named in one slot of b (b itself included); elsewhere any box. `near_mask`: 1 exactly where the slot names a cell inside the grid; at least one slot of every box is 0.
All inputs are finite; a program needn't handle non-finite values.
Results may differ from a plain program's by a relative error of at most 0.0027.
Values may be sent and summed in bfloat16 or wider, within the bound.
A program may use at most 128 MiB of HBM per device.

v0:
```python
import functools

import jax
import jax.numpy as jnp
import numpy as np
from jax import lax
from jax.experimental import pallas as pl
from jax.experimental.pallas import tpu as pltpu
from jax.sharding import PartitionSpec as P

MESH = pl.DeviceIdType.MESH
BF = jnp.bfloat16
F32 = jnp.float32

NB = 64
PER = 4
KD = 8
RHS = 32
SLOTS = 14
SZ = 256

ZX = 0
P1 = 1
F1 = 5
P2 = 7
F2 = 23
SIB = 31
HALF = 47
OFFS = (0, -1, 1, 2)


def input_order():
    order = np.zeros(256, np.int32)
    for w in range(2):
        for j in range(128):
            h, c, p2, p1, z = j // 64, j // 32 % 2, j // 8 % 4, j // 2 % 4, j % 2
            y, x = (p2, p1) if h == 0 else (p1, p2)
            order[w * 128 + j] = (((y * 2 + z) * 4 + x) * 2 + c) * 4 + 2 * h + w
    return order


def output_order():
    return np.array([4 * d + q for q in range(4) for d in range(64)], np.int32)


def dot_nt(a, b):
    return lax.dot_general(a, b, (((1,), (1,)), ((), ())), preferred_element_type=F32)


def body(idx_ref, src_ref, enc_ref, ker_ref, dec_ref, cols_ref, nb_hbm, out_ref,
         S, W, TT, D, V, SEND, R, NBV, NEAR, PS, PR, QI, QO,
         ssem, rsem, lsem, nsem, a2s, a2r, pss, psr):
    bi = lax.axis_index("box")
    zl = lax.axis_index("dir")
    c = lax.rem(bi, 2)
    x = lax.rem(bi // 2, 4)
    zh = lax.rem(bi // 8, 2)
    y = bi // 16

    def dev(y_, zh_, x_, c_):
        return ((y_ * 2 + zh_) * 4 + x_) * 2 + c_

    def wrap(v):
        return lax.rem(v + 8, 4)

    zpart = (dev(y, 1 - zh, x, c), 1 - zl)
    sib = (dev(y, zh, x, 1 - c), zl)
    partner = (bi, 1 - zl)

    nb_copies = [pltpu.make_async_copy(nb_hbm.at[q], NBV.at[q], nsem.at[q]) for q in range(PER)]
    for cp in nb_copies:
        cp.start()

    bar = pltpu.get_barrier_semaphore()

    def greet(t, _):
        pl.semaphore_signal(bar, inc=1, device_id=(lax.rem(bi + t, NB), zl), device_id_type=MESH)
        return 0

    lax.fori_loop(1, NB, greet, 0)
    pl.semaphore_signal(bar, inc=1, device_id=zpart, device_id_type=MESH)
    pl.semaphore_signal(bar, inc=1, device_id=partner, device_id_type=MESH)
    pl.semaphore_wait(bar, NB + 1)

    def pos(h):
        return (x, y) if h == 0 else (y, x)

    def ring(h, level, side):
        step = 1 if side == 0 else -1
        along_x = (h == 0) == (level == 1)
        if along_x:
            return (dev(y, zh, wrap(x + step), c), zl)
        return (dev(wrap(y + step), zh, x, c), zl)

    def sub(h, c_, p2, p1, z):
        return h * 64 + c_ * 32 + p2 * 8 + p1 * 2 + z

    def zof(which):
        return zh if which == 0 else 1 - zh

    def at(j, n=1):
        return S.at[pl.ds(2 * j, 2 * n)]

    started = []

    def send(h, num, j, device, n=1, src=None):
        cp = pltpu.make_async_remote_copy(
            src_ref=at(j, n) if src is None else src, dst_ref=at(j, n),
            send_sem=ssem.at[h * HALF + num], recv_sem=rsem.at[h * HALF + num],
            device_id=device, device_id_type=MESH)
        cp.start()
        started.append(cp)

    def recv(h, num, n=1):
        k = h * HALF + num
        pltpu.make_async_copy(S.at[pl.ds(0, 2 * n)], S.at[pl.ds(0, 2 * n)], rsem.at[k]).wait()

    def p2_send(h, piece, which, src=None):
        a, b = pos(h)
        j = sub(h, c, b, wrap(a + OFFS[piece]), zof(which))
        for side in (0, 1):
            send(h, P2 + 4 * piece + 2 * which + side, j, ring(h, 2, side), src=src)

    def encode(j0):
        rows = S[pl.ds(2 * j0, 4)].reshape(256, SZ)
        o = dot_nt(enc_ref[...], rows)
        top, low = o[0:8], o[8:16]
        lane = lax.broadcasted_iota(jnp.int32, (8, 128), 1) % 64
        for half in range(2):
            t = top[:, 128 * half:128 * half + 128]
            u = low[:, 128 * half:128 * half + 128]
            turned = jnp.where(lane < 32, -pltpu.roll(u, 96, 1), pltpu.roll(u, 32, 1))
            W[pl.ds(pl.multiple_of(8 * j0 + 8 * half, 8), 8), :] = t + turned

    def sib_send(h, drow, piece):
        a, b = pos(h)
        j0 = sub(h, c, wrap(b + OFFS[drow]), wrap(a + OFFS[piece]), 0)
        send(h, SIB + 4 * drow + piece, j0, sib, n=2)
        encode(j0)

    def p1_recv(h, which, side):
        recv(h, P1 + 2 * which + side)

    local = []
    for h in (0, 1):
        a, b = pos(h)
        own = sub(h, c, b, a, zh)
        src = src_ref.at[pl.ds(2 * h, 2)]
        send(h, ZX, own, zpart, src=src)
        for side in (0, 1):
            send(h, P1 + side, own, ring(h, 1, side), src=src)
        p2_send(h, 0, 0, src=src)
        cp = pltpu.make_async_copy(src, at(own), lsem.at[h])
        cp.start()
        local.append(cp)

    S[pl.ds(256, 2)] = jnp.zeros((2, 64, SZ), BF)
    cin = cols_ref[:, 0:1]
    cout = cols_ref[:, 1:2]
    QI[...] = jnp.where(lax.broadcasted_iota(jnp.int32, (256, 256), 1) == cin, 1.0, 0.0).astype(BF)
    QO[...] = jnp.where(lax.broadcasted_iota(jnp.int32, (256, 512), 1) == cout, 1.0, 0.0).astype(BF)

    def build_d(mine):
        col = pl.multiple_of(128 * (zl if mine else 1 - zl), 128)
        dr = dec_ref[0, :, pl.ds(col, 128)].astype(F32).reshape(64, 1, 8, 128)
        di = dec_ref[1, :, pl.ds(col, 128)].astype(F32).reshape(64, 1, 8, 128)
        left = jnp.concatenate([dr, -di], axis=1).reshape(1024, 128)
        right = jnp.concatenate([di, dr], axis=1).reshape(1024, 128)
        D[0 if mine else 1] = jnp.concatenate([left, right], axis=1).astype(BF)

    def build_t(k):
        d_i = lax.broadcasted_iota(jnp.int32, (16, 128), 0)
        l_i = lax.broadcasted_iota(jnp.int32, (16, 128), 1)
        ly, lz = l_i // 8, l_i % 8
        near = (((d_i <= 1) | (d_i == 15)) & ((ly <= 1) | (ly == 15)) & ((lz <= 1) | (lz == 7)))
        lane = lax.broadcasted_iota(jnp.int32, (8, 128), 1)
        for ri in range(2):
            row = jnp.where(near, 0.0, ker_ref[k, ri])
            row = jnp.where(lz < 4, row, pltpu.roll(row, 120, 1))
            pieces = {}
            for dx in range(-7, 8):
                base = jnp.broadcast_to(row[dx % 16:dx % 16 + 1, :], (8, 128))
                pieces[dx] = [pltpu.roll(base, sz, 1, stride=8, stride_axis=0) for sz in range(4)]
            pairs = {}
            for d in range(-7, 7):
                pairs[d] = [jnp.where(lane < 64, pieces[d][s], pltpu.roll(pieces[d + 1][s], 64, 1))
                            for s in range(4)]
            wide = jnp.concatenate([
                jnp.concatenate([pairs[2 * j - sx][s] for j in range(4)], axis=1)
                for sx in range(8) for s in range(4)], axis=0)
            hi = wide.astype(BF)
            lo = (wide - hi.astype(F32)).astype(BF)
            for part, val in enumerate((hi, lo)):
                first = dot_nt(QO[...], val).astype(BF)
                TT[k, part, ri] = dot_nt(first, QI[...]).astype(BF)

    build_d(False)
    build_d(True)
    for cp in local:
        cp.wait()

    for h in (0, 1):
        a, b = pos(h)
        recv(h, ZX)
        other = sub(h, c, b, a, 1 - zh)
        for side in (0, 1):
            send(h, P1 + 2 + side, other, ring(h, 1, side))
        p2_send(h, 0, 1)
        sib_send(h, 0, 0)

    for h in (0, 1):
        a, b = pos(h)
        for side in (0, 1):
            p1_recv(h, 0, side)
        send(h, F1, sub(h, c, b, wrap(a - 1), zh), ring(h, 1, 0))
        p2_send(h, 1, 0)
        p2_send(h, 2, 0)

    def step_t(k, _):
        build_t(k)
        return 0

    lax.fori_loop(0, 2, step_t, 0)

    for h in (0, 1):
        a, b = pos(h)
        for side in (0, 1):
            recv(h, P2 + side)
        send(h, F2, sub(h, c, wrap(b - 1), a, zh), ring(h, 2, 0))

    for h in (0, 1):
        a, b = pos(h)
        for side in (0, 1):
            p1_recv(h, 1, side)
        send(h, F1 + 1, sub(h, c, b, wrap(a + 1), 1 - zh), ring(h, 1, 1))
        p2_send(h, 1, 1)
        p2_send(h, 2, 1)
        sib_send(h, 0, 1)
        sib_send(h, 0, 2)

    lax.fori_loop(2, 4, step_t, 0)

    for h in (0, 1):
        a, b = pos(h)
        for side in (0, 1):
            recv(h, P2 + 2 + side)
        send(h, F2 + 1, sub(h, c, wrap(b + 1), a, 1 - zh), ring(h, 2, 1))
        sib_send(h, 1, 0)
        sib_send(h, 2, 0)

    for h in (0, 1):
        for side in (0, 1):
            recv(h, F1 + side)
        p2_send(h, 3, 0)
        p2_send(h, 3, 1)
        sib_send(h, 0, 3)

    lax.fori_loop(4, 6, step_t, 0)

    def relay(h, piece):
        a, b = pos(h)
        p1 = wrap(a + OFFS[piece])
        for which in (0, 1):
            for side in (0, 1):
                recv(h, P2 + 4 * piece + 2 * which + side)
            if which == 0:
                send(h, F2 + 2 * piece, sub(h, c, wrap(b - 1), p1, zh), ring(h, 2, 0))
            else:
                send(h, F2 + 2 * piece + 1, sub(h, c, wrap(b + 1), p1, 1 - zh), ring(h, 2, 1))
        sib_send(h, 1, piece)
        sib_send(h, 2, piece)

    for piece in (1, 2):
        for h in (0, 1):
            relay(h, piece)
    lax.fori_loop(6, 8, step_t, 0)
    for h in (0, 1):
        relay(h, 3)

    for piece in range(4):
        for h in (0, 1):
            for side in (0, 1):
                recv(h, F2 + 2 * piece + side)
            sib_send(h, 3, piece)

    for drow in range(4):
        for piece in range(4):
            for h in (0, 1):
                a, b = pos(h)
                recv(h, SIB + 4 * drow + piece, n=2)
                encode(sub(h, 1 - c, wrap(b + OFFS[drow]), wrap(a + OFFS[piece]), 0))

    for cp in started:
        cp.wait_send()

    lane64 = lax.broadcasted_iota(jnp.int32, (256, 64), 1)
    quarter = lax.broadcasted_iota(jnp.int32, (64, 128), 1) // 32

    def translate(k, _):
        v = W[pl.ds(k, 128, stride=8), :]
        e = jnp.concatenate([v[:, 0:64], v[:, 64:128]], axis=0)
        hi = e.astype(BF)
        lo = (e - hi.astype(F32)).astype(BF)
        t_hi = TT[k, 0].reshape(512, 256)
        t_lo = TT[k, 1].reshape(512, 256)
        nn = (((1,), (0,)), ((), ()))
        f = lax.dot_general(t_hi, hi, nn, preferred_element_type=F32)
        f = f + lax.dot_general(t_hi, lo, nn, preferred_element_type=F32)
        f = f + lax.dot_general(t_lo, hi, nn, preferred_element_type=F32)
        fr, fi = f[0:256], f[256:512]
        swapped = jnp.concatenate([fi[:, 32:64], fi[:, 0:32]], axis=1)
        far = fr + jnp.where(lane64 < 32, -swapped, swapped)
        far = jnp.concatenate([far, far], axis=1)
        far_sw = pltpu.roll(far, 32, 1)
        for ri in range(2):
            val = None
            for q in range(4):
                use = far if (q - ri) % 2 == 0 else far_sw
                block = use[64 * q:64 * q + 64]
                val = block if val is None else jnp.where(quarter == q, block, val)
            V[pl.ds(8 * ri + k, 64, stride=16), :] = val
        return 0

    lax.fori_loop(0, KD, translate, 0)
    SEND[...] = V[...].astype(BF).reshape(64, 16, 128)
    R[pl.ds(bi, 1)] = SEND[pl.ds(bi, 1)]

    def scatter(t, _):
        dst = lax.rem(bi + t, NB)
        pltpu.make_async_remote_copy(
            src_ref=SEND.at[dst], dst_ref=R.at[bi], send_sem=a2s.at[0], recv_sem=a2r.at[0],
            device_id=(dst, zl), device_id_type=MESH).start()
        return 0

    lax.fori_loop(1, NB, scatter, 0)

    def near_box(q, _):
        blocks = NBV[q]
        xs = jnp.concatenate([S[idx_ref[q, s]] for s in range(SLOTS)], axis=1)
        bs = jnp.concatenate([blocks[s] for s in range(SLOTS)], axis=1)
        n = dot_nt(xs, bs)
        NEAR[q, 0] = n[0:32, 0:256] - n[32:64, 256:512]
        NEAR[q, 1] = n[32:64, 0:256] + n[0:32, 256:512]
        return 0

    for cp in nb_copies:
        cp.wait()
    lax.fori_loop(0, PER, near_box, 0)

    whole = R.at[pl.ds(0, NB - 1)]
    pltpu.make_async_copy(whole, whole, a2r.at[0]).wait()
    got = R[...].reshape(1024, 128)

    def decode(which):
        return lax.dot_general(got, D[which], (((0,), (0,)), ((), ())), preferred_element_type=F32)

    def combine(which, target):
        far = decode(which)
        col = pl.multiple_of(128 * (zl if which == 0 else 1 - zl), 128)
        for q in range(4):
            for ro in range(2):
                target[q, ro] = (far[32 * q:32 * q + 32, 128 * ro:128 * ro + 128]
                                 + NEAR[q, ro, :, pl.ds(col, 128)])

    combine(1, PS)
    last = pltpu.make_async_remote_copy(
        src_ref=PS, dst_ref=PR, send_sem=pss.at[0], recv_sem=psr.at[0],
        device_id=partner, device_id_type=MESH)
    last.start()
    combine(0, out_ref)
    sent = SEND.at[pl.ds(0, NB - 1)]
    pltpu.make_async_copy(sent, sent, a2s.at[0]).wait()
    last.wait()
    out_ref[...] += PR[...]


def on_device(sources, encode, kernel, decode, near_blocks, near_list, near_mask, box_cell):
    bi = lax.axis_index("box")
    enc = lax.dynamic_slice_in_dim(encode, bi * KD, KD, axis=1).reshape(2 * KD, SZ)
    v = near_list
    w, h, c = v % 2, v // 2 % 2, v // 4 % 2
    x, z, y = v // 8 % 4, v // 32 % 2, v // 64
    p2 = jnp.where(h == 1, x, y)
    p1 = jnp.where(h == 1, y, x)
    idx = 2 * (h * 64 + c * 32 + p2 * 8 + p1 * 2 + z) + w
    idx = jnp.where(near_mask == 1, idx, 256)
    cx, cy, cz = box_cell // 32, box_cell // 4 % 8, box_cell % 4
    cell_in = cx * 32 + cz * 8 + cy
    cell_out = cx * 64 + cy * 8 + cz
    cols = jnp.stack([cell_in[input_order()], cell_out[output_order()]], axis=1)
    vm = pl.BlockSpec(memory_space=pltpu.VMEM)
    n_sem = 2 * HALF
    return pl.pallas_call(
        body,
        out_shape=jax.ShapeDtypeStruct((PER, 2, RHS, 128), F32),
        in_specs=[pl.BlockSpec(memory_space=pltpu.SMEM), vm, vm, vm, vm, vm,
                  pl.BlockSpec(memory_space=pl.ANY)],
        out_specs=vm,
        scratch_shapes=[
            pltpu.VMEM((258, 64, SZ), BF),
            pltpu.VMEM((1024, 128), F32),
            pltpu.VMEM((KD, 2, 2, 256, 256), BF),
            pltpu.VMEM((2, 1024, 256), BF),
            pltpu.VMEM((1024, 128), F32),
            pltpu.VMEM((NB, 16, 128), BF),
            pltpu.VMEM((NB, 16, 128), BF),
            pltpu.VMEM((PER, SLOTS, 512, SZ), BF),
            pltpu.VMEM((PER, 2, RHS, SZ), F32),
            pltpu.VMEM((PER, 2, RHS, 128), F32),
            pltpu.VMEM((PER, 2, RHS, 128), F32),
            pltpu.VMEM((256, 256), BF),
            pltpu.VMEM((256, 512), BF),
            pltpu.SemaphoreType.DMA((n_sem,)),
            pltpu.SemaphoreType.DMA((n_sem,)),
            pltpu.SemaphoreType.DMA((2,)),
            pltpu.SemaphoreType.DMA((PER,)),
            pltpu.SemaphoreType.DMA((1,)),
            pltpu.SemaphoreType.DMA((1,)),
            pltpu.SemaphoreType.DMA((1,)),
            pltpu.SemaphoreType.DMA((1,)),
        ],
        compiler_params=pltpu.CompilerParams(
            collective_id=0, has_side_effects=True, vmem_limit_bytes=56 * 2**20),
        name="fmm",
    )(idx, sources.reshape(PER, 64, SZ), enc, kernel, decode, cols,
      near_blocks.reshape(PER, SLOTS, 512, SZ))


def solution(mesh):
    in_specs = (
        P("box", None, None, None),
        P(None, "dir", None),
        P(("dir", "box"), None, None, None),
        P(None, "dir", None),
        P("box", "dir", None, None, None),
        P("box", "dir"),
        P("box", "dir"),
        P(),
    )
    return jax.shard_map(
        on_device, mesh=mesh, in_specs=in_specs, out_specs=P("box", None, None, "dir"),
        check_vma=False)
```

profile of v0, /device:TPU:1, one launch (start us, length us, event | category | flops | bytes accessed | tf_op | source)
XLA Modules:
  0.0 78.5 jit_solution(12808738759979946393)
XLA Ops:
  0.0 0.0 copy-start
  0.0 1.4 %fusion.10.idx_ref = s32[4,14]{1,0:T(4,128)} fusion(s32[4,14]{1,0:T(4,128)} %param.17, s32[4,14]{1,0:T(4,128)} %param.18), kind=kLoop, calls=%fused_computation.46 | loop fusion | flops 6608 | bytes 672 | tf_op jit(solution)/shard_map/jit(_where)/select_n | solution.py:386
  1.4 0.7 add_add_fusion.1
  2.1 0.7 add_add_fusion
  2.7 0.7 pad_clamp_fusion.1
  3.4 1.9 %gather_fusion = s32[256]{0:T(256)S(1)} fusion(s32[256]{0:T(256)S(1)} %get-tuple-element.5, s32[1024]{0:T(1024)S(1)} %pad_clamp_fusion.1), kind=kCustom, calls=%fused_computation | custom fusion | bytes 3072 | tf_op jit(solution)/shard_map/gather | solution.py:390
  5.4 0.7 pad_clamp_fusion
  6.1 1.9 %gather_fusion.1 = s32[256]{0:T(256)S(1)} fusion(s32[256]{0:T(256)S(1)} %add_add_fusion, s32[1024]{0:T(1024)S(1)} %pad_clamp_fusion), kind=kCustom, calls=%fused_computation.1 | custom fusion | bytes 3072 | tf_op jit(solution)/shard_map/gather | solution.py:390
  8.0 0.0 copy-done
  8.0 0.6 dynamic-slice_bitcast_fusion.enc_ref
  8.7 0.8 %copy.15.cols_ref = s32[256,2]{1,0:T(8,128)} copy(s32[256,2]{0,1:T(2,128)S(1)} %pad_add_fusion) | data formatting | bytes 4096 | tf_op jit(solution)/shard_map/stack | solution.py:390
  9.4 67.5 %fmm.1 = f32[4,2,32,128]{3,2,1,0:T(8,128)} custom-call(s32[4,14]{1,0:T(4,128)} %fusion.10.idx_ref, bf16[4,64,256]{2,1,0:T(8,128)(2,1)} %bitcast.7, bf16[16,256]{1,0:T(8,128)(2,1)} %dynamic-slice_bitcast_fusion.enc_ref, f32[8,2,16,128]{3,2,1,0:T(8,128)} %ker_ref.1, bf16[2,512,256]{2,1,0:T(8,128)(2,1)} %dec_ref.1, s32[256,2]{1,0:T(8,128)} %copy.15.cols_ref, ...), custom_call_target="tpu_custom_call" | custom-call | tf_op jit(solution)/shard_map/fmm/pallas_call | solution.py:393
  76.9 1.6 %copy.17 = f32[4,2,32,128]{3,2,1,0:T(8,128)} copy(f32[4,2,32,128]{3,2,1,0:T(8,128)} %fmm.1) | data formatting | bytes 262144
  (1 shorter events, 0.0 us)
Async XLA Ops:
  0.0 8.0 %copy-start = (bf16[2,512,256]{2,1,0:T(8,128)(2,1)S(1)}, bf16[2,512,256]{2,1,0:T(8,128)(2,1)}, u32[]{:S(2)}) copy-start(bf16[2,512,256]{2,1,0:T(8,128)(2,1)} %param.13) | copy-start | bytes 1572868
where the time goes:
time: 78.7 us; the launch traced here: 78.5 us
  Pallas kernels  67.5 us (86%)
  local copies, waits for them, and re-layouts  6.86 us (9%)
  other arithmetic  4.12 us (5%)
    pallas_call x1, Pallas kernels, on_device(): pl.pallas_call(body, out_shape=jax.ShapeDtypeStruct((PER, 2, RHS, 128), F...  67.5 us
    gather x2, local copies, waits for them, and re-layouts, on_device(): cols = jnp.stack([cell_in[input_order()], cell_out[output_order()]], axis=1)  3.88 us

commit v1 on v0

--- a/solution.py
+++ b/solution.py
@@ -1,8 +1,5 @@
-import functools
-
 import jax
 import jax.numpy as jnp
-import numpy as np
 from jax import lax
 from jax.experimental import pallas as pl
 from jax.experimental.pallas import tpu as pltpu
@@ -29,27 +26,29 @@
 OFFS = (0, -1, 1, 2)
 
 
-def input_order():
-    order = np.zeros(256, np.int32)
-    for w in range(2):
-        for j in range(128):
-            h, c, p2, p1, z = j // 64, j // 32 % 2, j // 8 % 4, j // 2 % 4, j % 2
-            y, x = (p2, p1) if h == 0 else (p1, p2)
-            order[w * 128 + j] = (((y * 2 + z) * 4 + x) * 2 + c) * 4 + 2 * h + w
-    return order
-
-
-def output_order():
-    return np.array([4 * d + q for q in range(4) for d in range(64)], np.int32)
+def box_of_input(i):
+    w, j = i // 128, i % 128
+    h, c, p2, p1, z = j // 64, j // 32 % 2, j // 8 % 4, j // 2 % 4, j % 2
+    y = jnp.where(h == 0, p2, p1)
+    x = jnp.where(h == 0, p1, p2)
+    return (((y * 2 + z) * 4 + x) * 2 + c) * 4 + 2 * h + w
+
+
+def slot_of_box(v):
+    w, h, c = lax.rem(v, 2), lax.rem(v // 2, 2), lax.rem(v // 4, 2)
+    x, z, y = lax.rem(v // 8, 4), lax.rem(v // 32, 2), v // 64
+    first = 8 * y + 2 * x
+    second = 8 * x + 2 * y
+    return 2 * (h * 64 + c * 32 + jnp.where(h == 1, second, first) + z) + w
 
 
 def dot_nt(a, b):
     return lax.dot_general(a, b, (((1,), (1,)), ((), ())), preferred_element_type=F32)
 
 
-def body(idx_ref, src_ref, enc_ref, ker_ref, dec_ref, cols_ref, nb_hbm, out_ref,
-         S, W, TT, D, V, SEND, R, NBV, NEAR, PS, PR, QI, QO,
-         ssem, rsem, lsem, nsem, a2s, a2r, pss, psr):
+def body(list_ref, mask_ref, cell_ref, src_ref, enc_hbm, ker_hbm, dec_hbm, nb_hbm, out_ref,
+         S, W, TT, D, V, SEND, R, NBV, NEAR, NS, NR, FS, FR, QI, QO, BASE, ENC2, E16, KER, DEC,
+         ssem, rsem, lsem, nsem, isem, a2s, a2r, pss, psr, ready):
     bi = lax.axis_index("box")
     zl = lax.axis_index("dir")
     c = lax.rem(bi, 2)
@@ -67,20 +66,22 @@
     sib = (dev(y, zh, x, 1 - c), zl)
     partner = (bi, 1 - zl)
 
+    right, left = (dev(y, zh, wrap(x + 1), c), zl), (dev(y, zh, wrap(x - 1), c), zl)
+    up, down = (dev(wrap(y + 1), zh, x, c), zl), (dev(wrap(y - 1), zh, x, c), zl)
+    bar = pltpu.get_barrier_semaphore()
+    for other in (right, left, up, down, zpart, sib, partner):
+        pl.semaphore_signal(bar, inc=1, device_id=other, device_id_type=MESH)
+
+    in_copies = [
+        pltpu.make_async_copy(enc_hbm.at[:, pl.ds(pl.multiple_of(16 * (bi // 2), 16), 16), :], ENC2, isem.at[0]),
+        pltpu.make_async_copy(ker_hbm, KER, isem.at[1]),
+        pltpu.make_async_copy(dec_hbm, DEC, isem.at[2])]
+    for cp in in_copies:
+        cp.start()
     nb_copies = [pltpu.make_async_copy(nb_hbm.at[q], NBV.at[q], nsem.at[q]) for q in range(PER)]
     for cp in nb_copies:
         cp.start()
-
-    bar = pltpu.get_barrier_semaphore()
-
-    def greet(t, _):
-        pl.semaphore_signal(bar, inc=1, device_id=(lax.rem(bi + t, NB), zl), device_id_type=MESH)
-        return 0
-
-    lax.fori_loop(1, NB, greet, 0)
-    pl.semaphore_signal(bar, inc=1, device_id=zpart, device_id_type=MESH)
-    pl.semaphore_signal(bar, inc=1, device_id=partner, device_id_type=MESH)
-    pl.semaphore_wait(bar, NB + 1)
+    pl.semaphore_wait(bar, 7)
 
     def pos(h):
         return (x, y) if h == 0 else (y, x)
@@ -123,7 +124,7 @@
 
     def encode(j0):
         rows = S[pl.ds(2 * j0, 4)].reshape(256, SZ)
-        o = dot_nt(enc_ref[...], rows)
+        o = dot_nt(E16[...], rows)
         top, low = o[0:8], o[8:16]
         lane = lax.broadcasted_iota(jnp.int32, (8, 128), 1) % 64
         for half in range(2):
@@ -155,38 +156,62 @@
         local.append(cp)
 
     S[pl.ds(256, 2)] = jnp.zeros((2, 64, SZ), BF)
-    cin = cols_ref[:, 0:1]
-    cout = cols_ref[:, 1:2]
-    QI[...] = jnp.where(lax.broadcasted_iota(jnp.int32, (256, 256), 1) == cin, 1.0, 0.0).astype(BF)
-    QO[...] = jnp.where(lax.broadcasted_iota(jnp.int32, (256, 512), 1) == cout, 1.0, 0.0).astype(BF)
+    cell = cell_ref[...]
+    cx, cy, cz = cell // 32, cell // 4 % 8, cell % 4
+    cell_in = cx * 32 + cz * 8 + cy
+    row = lax.broadcasted_iota(jnp.int32, (256, 256), 0)
+    col = lax.broadcasted_iota(jnp.int32, (256, 256), 1)
+    row1 = lax.broadcasted_iota(jnp.int32, (256, 1), 0)
+
+    def hot(cond):
+        return jnp.where(cond, 1.0, 0.0).astype(BF)
+
+    QI[...] = dot_nt(hot(box_of_input(row1) == col), hot(row == cell_in)).astype(BF)
+    QO[...] = dot_nt(hot(4 * (row1 % 64) + row1 // 64 == col), hot(row == cell)).astype(BF)
+
+    in_copies[0].wait()
+    pair = ENC2[...].astype(F32)
+    E16[...] = jnp.where(lax.rem(bi, 2) == 1, pair[:, 8:16], pair[:, 0:8]).reshape(16, SZ).astype(BF)
+
+    in_copies[1].wait()
+    d_i = lax.broadcasted_iota(jnp.int32, (256, 128), 0) % 16
+    l_i = lax.broadcasted_iota(jnp.int32, (256, 128), 1)
+    ly, lz = l_i // 8, l_i % 8
+    close = (((d_i <= 1) | (d_i == 15)) & ((ly <= 1) | (ly == 15)) & ((lz <= 1) | (lz == 7)))
+    kept = jnp.where(close, 0.0, KER[...].reshape(256, 128))
+    k_hi = kept.astype(BF)
+    k_lo = (kept - k_hi.astype(F32)).astype(BF)
+    lane512 = lax.broadcasted_iota(jnp.int32, (128, 512), 1)
+    take = (lane512 % 64) // 4 * 8 + (lane512 % 4 - lane512 // 128 + 8) % 8
+    spread = hot(lax.broadcasted_iota(jnp.int32, (128, 512), 0) == take)
+    BASE[...] = (jnp.dot(k_hi, spread, preferred_element_type=F32)
+                 + jnp.dot(k_lo, spread, preferred_element_type=F32))
 
     def build_d(mine):
         col = pl.multiple_of(128 * (zl if mine else 1 - zl), 128)
-        dr = dec_ref[0, :, pl.ds(col, 128)].astype(F32).reshape(64, 1, 8, 128)
-        di = dec_ref[1, :, pl.ds(col, 128)].astype(F32).reshape(64, 1, 8, 128)
+        dr = DEC[0, :, pl.ds(col, 128)].astype(F32).reshape(64, 1, 8, 128)
+        di = DEC[1, :, pl.ds(col, 128)].astype(F32).reshape(64, 1, 8, 128)
         left = jnp.concatenate([dr, -di], axis=1).reshape(1024, 128)
         right = jnp.concatenate([di, dr], axis=1).reshape(1024, 128)
         D[0 if mine else 1] = jnp.concatenate([left, right], axis=1).astype(BF)
 
+    lane = lax.broadcasted_iota(jnp.int32, (8, 128), 1)
+
     def build_t(k):
-        d_i = lax.broadcasted_iota(jnp.int32, (16, 128), 0)
-        l_i = lax.broadcasted_iota(jnp.int32, (16, 128), 1)
-        ly, lz = l_i // 8, l_i % 8
-        near = (((d_i <= 1) | (d_i == 15)) & ((ly <= 1) | (ly == 15)) & ((lz <= 1) | (lz == 7)))
-        lane = lax.broadcasted_iota(jnp.int32, (8, 128), 1)
         for ri in range(2):
-            row = jnp.where(near, 0.0, ker_ref[k, ri])
-            row = jnp.where(lz < 4, row, pltpu.roll(row, 120, 1))
-            pieces = {}
+            rows = BASE[pl.ds(pl.multiple_of(32 * k + 16 * ri, 16), 16), :]
+            one, two = {}, {}
             for dx in range(-7, 8):
-                base = jnp.broadcast_to(row[dx % 16:dx % 16 + 1, :], (8, 128))
-                pieces[dx] = [pltpu.roll(base, sz, 1, stride=8, stride_axis=0) for sz in range(4)]
-            pairs = {}
+                line = rows[dx % 16:dx % 16 + 1, :]
+                one[dx] = [pltpu.roll(jnp.broadcast_to(line[:, 128 * s:128 * s + 128], (8, 128)),
+                                      0, 1, stride=4, stride_axis=0) for s in range(4)]
             for d in range(-7, 7):
-                pairs[d] = [jnp.where(lane < 64, pieces[d][s], pltpu.roll(pieces[d + 1][s], 64, 1))
-                            for s in range(4)]
+                two[d] = [jnp.where(lane % 64 < 32, one[d][s], pltpu.roll(one[d + 1][s], 32, 1))
+                          for s in range(4)]
+            four = {d: [jnp.where(lane < 64, two[d][s], two[d + 2][s]) for s in range(4)]
+                    for d in range(-7, 5)}
             wide = jnp.concatenate([
-                jnp.concatenate([pairs[2 * j - sx][s] for j in range(4)], axis=1)
+                jnp.concatenate([four[-sx][s], four[4 - sx][s]], axis=1)
                 for sx in range(8) for s in range(4)], axis=0)
             hi = wide.astype(BF)
             lo = (wide - hi.astype(F32)).astype(BF)
@@ -194,11 +219,17 @@
                 first = dot_nt(QO[...], val).astype(BF)
                 TT[k, part, ri] = dot_nt(first, QI[...]).astype(BF)
 
+    def step_t(k):
+        lax.fori_loop(k, k + 1, lambda n, _: (build_t(n), 0)[1], 0)
+
+    in_copies[2].wait()
     build_d(False)
     build_d(True)
     for cp in local:
         cp.wait()
 
+    step_t(0)
+
     for h in (0, 1):
         a, b = pos(h)
         recv(h, ZX)
@@ -216,17 +247,15 @@
         p2_send(h, 1, 0)
         p2_send(h, 2, 0)
 
-    def step_t(k, _):
-        build_t(k)
-        return 0
-
-    lax.fori_loop(0, 2, step_t, 0)
+    step_t(1)
 
     for h in (0, 1):
         a, b = pos(h)
         for side in (0, 1):
             recv(h, P2 + side)
         send(h, F2, sub(h, c, wrap(b - 1), a, zh), ring(h, 2, 0))
+
+    step_t(2)
 
     for h in (0, 1):
         a, b = pos(h)
@@ -238,7 +267,7 @@
         sib_send(h, 0, 1)
         sib_send(h, 0, 2)
 
-    lax.fori_loop(2, 4, step_t, 0)
+    step_t(3)
 
     for h in (0, 1):
         a, b = pos(h)
@@ -248,6 +277,8 @@
         sib_send(h, 1, 0)
         sib_send(h, 2, 0)
 
+    step_t(4)
+
     for h in (0, 1):
         for side in (0, 1):
             recv(h, F1 + side)
@@ -255,7 +286,7 @@
         p2_send(h, 3, 1)
         sib_send(h, 0, 3)
 
-    lax.fori_loop(4, 6, step_t, 0)
+    step_t(5)
 
     def relay(h, piece):
         a, b = pos(h)
@@ -273,7 +304,7 @@
     for piece in (1, 2):
         for h in (0, 1):
             relay(h, piece)
-    lax.fori_loop(6, 8, step_t, 0)
+        step_t(5 + piece)
     for h in (0, 1):
         relay(h, 3)
 
@@ -290,6 +321,7 @@
                 recv(h, SIB + 4 * drow + piece, n=2)
                 encode(sub(h, 1 - c, wrap(b + OFFS[drow]), wrap(a + OFFS[piece]), 0))
 
+    pl.semaphore_signal(ready, inc=1, device_id=partner, device_id_type=MESH)
     for cp in started:
         cp.wait_send()
 
@@ -332,11 +364,14 @@
             device_id=(dst, zl), device_id_type=MESH).start()
         return 0
 
+    pl.semaphore_wait(ready, 1)
     lax.fori_loop(1, NB, scatter, 0)
 
     def near_box(q, _):
         blocks = NBV[q]
-        xs = jnp.concatenate([S[idx_ref[q, s]] for s in range(SLOTS)], axis=1)
+        xs = jnp.concatenate(
+            [S[jnp.where(mask_ref[q, s] == 1, slot_of_box(list_ref[q, s]), 256)]
+             for s in range(SLOTS)], axis=1)
         bs = jnp.concatenate([blocks[s] for s in range(SLOTS)], axis=1)
         n = dot_nt(xs, bs)
         NEAR[q, 0] = n[0:32, 0:256] - n[32:64, 256:512]
@@ -347,6 +382,14 @@
         cp.wait()
     lax.fori_loop(0, PER, near_box, 0)
 
+    mine = pl.multiple_of(128 * zl, 128)
+    theirs = pl.multiple_of(128 * (1 - zl), 128)
+    NS[...] = NEAR[:, :, :, pl.ds(theirs, 128)]
+    near_out = pltpu.make_async_remote_copy(
+        src_ref=NS, dst_ref=NR, send_sem=pss.at[0], recv_sem=psr.at[0],
+        device_id=partner, device_id_type=MESH)
+    near_out.start()
+
     whole = R.at[pl.ds(0, NB - 1)]
     pltpu.make_async_copy(whole, whole, a2r.at[0]).wait()
     got = R[...].reshape(1024, 128)
@@ -354,47 +397,34 @@
     def decode(which):
         return lax.dot_general(got, D[which], (((0,), (0,)), ((), ())), preferred_element_type=F32)
 
-    def combine(which, target):
-        far = decode(which)
-        col = pl.multiple_of(128 * (zl if which == 0 else 1 - zl), 128)
-        for q in range(4):
-            for ro in range(2):
-                target[q, ro] = (far[32 * q:32 * q + 32, 128 * ro:128 * ro + 128]
-                                 + NEAR[q, ro, :, pl.ds(col, 128)])
-
-    combine(1, PS)
-    last = pltpu.make_async_remote_copy(
-        src_ref=PS, dst_ref=PR, send_sem=pss.at[0], recv_sem=psr.at[0],
+    FS[...] = decode(1).astype(BF)
+    far_out = pltpu.make_async_remote_copy(
+        src_ref=FS, dst_ref=FR, send_sem=pss.at[1], recv_sem=psr.at[1],
         device_id=partner, device_id_type=MESH)
-    last.start()
-    combine(0, out_ref)
+    far_out.start()
+    far = decode(0)
+    near_out.wait()
+    for q in range(4):
+        for ro in range(2):
+            out_ref[q, ro] = (far[32 * q:32 * q + 32, 128 * ro:128 * ro + 128]
+                              + NEAR[q, ro, :, pl.ds(mine, 128)] + NR[q, ro])
     sent = SEND.at[pl.ds(0, NB - 1)]
     pltpu.make_async_copy(sent, sent, a2s.at[0]).wait()
-    last.wait()
-    out_ref[...] += PR[...]
+    far_out.wait()
+    for q in range(4):
+        for ro in range(2):
+            out_ref[q, ro] += FR[32 * q:32 * q + 32, 128 * ro:128 * ro + 128].astype(F32)
 
 
 def on_device(sources, encode, kernel, decode, near_blocks, near_list, near_mask, box_cell):
-    bi = lax.axis_index("box")
-    enc = lax.dynamic_slice_in_dim(encode, bi * KD, KD, axis=1).reshape(2 * KD, SZ)
-    v = near_list
-    w, h, c = v % 2, v // 2 % 2, v // 4 % 2
-    x, z, y = v // 8 % 4, v // 32 % 2, v // 64
-    p2 = jnp.where(h == 1, x, y)
-    p1 = jnp.where(h == 1, y, x)
-    idx = 2 * (h * 64 + c * 32 + p2 * 8 + p1 * 2 + z) + w
-    idx = jnp.where(near_mask == 1, idx, 256)
-    cx, cy, cz = box_cell // 32, box_cell // 4 % 8, box_cell % 4
-    cell_in = cx * 32 + cz * 8 + cy
-    cell_out = cx * 64 + cy * 8 + cz
-    cols = jnp.stack([cell_in[input_order()], cell_out[output_order()]], axis=1)
+    smem = pl.BlockSpec(memory_space=pltpu.SMEM)
+    hbm = pl.BlockSpec(memory_space=pl.ANY)
     vm = pl.BlockSpec(memory_space=pltpu.VMEM)
     n_sem = 2 * HALF
     return pl.pallas_call(
         body,
         out_shape=jax.ShapeDtypeStruct((PER, 2, RHS, 128), F32),
-        in_specs=[pl.BlockSpec(memory_space=pltpu.SMEM), vm, vm, vm, vm, vm,
-                  pl.BlockSpec(memory_space=pl.ANY)],
+        in_specs=[smem, smem, vm, hbm, hbm, hbm, hbm, hbm],
         out_specs=vm,
         scratch_shapes=[
             pltpu.VMEM((258, 64, SZ), BF),
@@ -408,22 +438,31 @@
             pltpu.VMEM((PER, 2, RHS, SZ), F32),
             pltpu.VMEM((PER, 2, RHS, 128), F32),
             pltpu.VMEM((PER, 2, RHS, 128), F32),
+            pltpu.VMEM((128, 256), BF),
+            pltpu.VMEM((128, 256), BF),
             pltpu.VMEM((256, 256), BF),
-            pltpu.VMEM((256, 512), BF),
+            pltpu.VMEM((256, 256), BF),
+            pltpu.VMEM((256, 512), F32),
+            pltpu.VMEM((2, 16, SZ), BF),
+            pltpu.VMEM((16, SZ), BF),
+            pltpu.VMEM((KD, 2, 16, 128), F32),
+            pltpu.VMEM((2, 512, SZ), BF),
             pltpu.SemaphoreType.DMA((n_sem,)),
             pltpu.SemaphoreType.DMA((n_sem,)),
             pltpu.SemaphoreType.DMA((2,)),
             pltpu.SemaphoreType.DMA((PER,)),
+            pltpu.SemaphoreType.DMA((3,)),
             pltpu.SemaphoreType.DMA((1,)),
             pltpu.SemaphoreType.DMA((1,)),
-            pltpu.SemaphoreType.DMA((1,)),
-            pltpu.SemaphoreType.DMA((1,)),
+            pltpu.SemaphoreType.DMA((2,)),
+            pltpu.SemaphoreType.DMA((2,)),
+            pltpu.SemaphoreType.REGULAR,
         ],
         compiler_params=pltpu.CompilerParams(
             collective_id=0, has_side_effects=True, vmem_limit_bytes=56 * 2**20),
         name="fmm",
-    )(idx, sources.reshape(PER, 64, SZ), enc, kernel, decode, cols,
-      near_blocks.reshape(PER, SLOTS, 512, SZ))
+    )(near_list, near_mask, box_cell.reshape(1, 256), sources.reshape(PER, 64, SZ), encode, kernel,
+      decode, near_blocks.reshape(PER, SLOTS, 512, SZ))
 
 
 def solution(mesh):

time: 78.7 us -> 62.1 us (0.79)
  Pallas kernels: 67.5 us -> 60.4 us
  local copies, waits for them, and re-layouts: 6.86 us -> 1.57 us
  other arithmetic: 4.12 us -> 0 us
    pallas_call x1, Pallas kernels: 67.5 us -> 60.4 us  [on_device(): pl.pallas_call(body, out_shape=jax.ShapeDtypeStruct((PER, 2, RHS, 128), F...]
    gather x2 -> x0, local copies, waits for them, and re-layouts: 3.88 us -> none  [on_device(): cols = jnp.stack([cell_in[input_order()], cell_out[output_order()]], axis=1)]
    add x2 -> x0, other arithmetic: 1.39 us -> none  [the longest x1 0.7 us: on_device(): cell_in = cx * 32 + cz * 8 + cy]
    gather x2 -> x0, other arithmetic: 1.37 us -> none  [on_device(): cols = jnp.stack([cell_in[input_order()], cell_out[output_order()]], axis=1)]
    select_n x1 -> x0, other arithmetic: 1.36 us -> none  [on_device(): idx = jnp.where(near_mask == 1, idx, 256)]
    another operation x1 -> x0, local copies, waits for them, and re-layouts: 0.8 us -> none  [on_device(): cols = jnp.stack([cell_in[input_order()], cell_out[output_order()]], axis=1)]
where the time goes in v1:
time: 62.1 us; the launch traced here: 62 us
  Pallas kernels  60.4 us (97%)
  local copies, waits for them, and re-layouts  1.57 us (3%)
    pallas_call x1, Pallas kernels, on_device(): pl.pallas_call(body, out_shape=jax.ShapeDtypeStruct((PER, 2, RHS, 128), F...  60.4 us
    unnamed x1, local copies, waits for them, and re-layouts  1.57 us

profile of v1, /device:TPU:1, one launch (start us, length us, event | category | flops | bytes accessed | tf_op | source)
XLA Modules:
  0.0 62.0 jit_solution(10601626594414316419)
XLA Ops:
  0.0 60.4 %fmm.1 = f32[4,2,32,128]{3,2,1,0:T(8,128)} custom-call(s32[4,14]{1,0:T(4,128)} %list_ref.1, s32[4,14]{1,0:T(4,128)} %mask_ref.1, s32[1,256]{1,0:T(1,128)} %bitcast.5, bf16[4,64,256]{2,1,0:T(8,128)(2,1)} %bitcast.4, bf16[2,512,256]{2,1,0:T(8,128)(2,1)} %enc_hbm.1, f32[8,2,16,128]{3,2,1,0:T(8,128)} %ker_hbm.1, bf16[2,512,256]{2,1,0:T(8,128)(2,1)} %dec_hbm.1, ...), custom_call_target="tpu_custom_call" | custom-call | tf_op jit(solution)/shard_map/fmm/pallas_call | solution.py:424
  60.4 1.6 %copy.10 = f32[4,2,32,128]{3,2,1,0:T(8,128)} copy(f32[4,2,32,128]{3,2,1,0:T(8,128)} %fmm.1) | data formatting | bytes 262144

commit v2 on v1

--- a/solution.py
+++ b/solution.py
@@ -22,7 +22,8 @@
 P2 = 7
 F2 = 23
 SIB = 31
-HALF = 47
+PX = 47
+HALF = 59
 OFFS = (0, -1, 1, 2)
 
 
@@ -104,23 +105,60 @@
 
     started = []
 
-    def send(h, num, j, device, n=1, src=None):
+    def copy(h, num, src, dst, device):
         cp = pltpu.make_async_remote_copy(
-            src_ref=at(j, n) if src is None else src, dst_ref=at(j, n),
+            src_ref=src, dst_ref=dst,
             send_sem=ssem.at[h * HALF + num], recv_sem=rsem.at[h * HALF + num],
             device_id=device, device_id_type=MESH)
         cp.start()
         started.append(cp)
 
-    def recv(h, num, n=1):
+    def send(h, num, j, device, n=1, src=None):
+        copy(h, num, at(j, n) if src is None else src, at(j, n), device)
+
+    def send_box(h, num, j, device, src=None):
+        one = S.at[pl.ds(2 * j + zl, 1)]
+        copy(h, num, one if src is None else src, one, device)
+
+    def recv(h, num, boxes=2):
         k = h * HALF + num
-        pltpu.make_async_copy(S.at[pl.ds(0, 2 * n)], S.at[pl.ds(0, 2 * n)], rsem.at[k]).wait()
+        pltpu.make_async_copy(S.at[pl.ds(0, boxes)], S.at[pl.ds(0, boxes)], rsem.at[k]).wait()
+
+    def spot(h, drow, piece, which):
+        a, b = pos(h)
+        return sub(h, c, wrap(b + OFFS[drow]), wrap(a + OFFS[piece]), zof(which))
 
     def p2_send(h, piece, which, src=None):
-        a, b = pos(h)
-        j = sub(h, c, b, wrap(a + OFFS[piece]), zof(which))
+        j = spot(h, 0, piece, which)
         for side in (0, 1):
-            send(h, P2 + 4 * piece + 2 * which + side, j, ring(h, 2, side), src=src)
+            num = P2 + 4 * piece + 2 * which + side
+            if piece < 2:
+                send_box(h, num, j, ring(h, 2, side), src)
+            else:
+                send(h, num, j, ring(h, 2, side), src=src)
+
+    def p2_recv(h, piece, which):
+        for side in (0, 1):
+            recv(h, P2 + 4 * piece + 2 * which + side, 1 if piece < 2 else 2)
+
+    def f2_send(h, piece, which):
+        j = spot(h, 1 if which == 0 else 2, piece, which)
+        num = F2 + 2 * piece + which
+        if piece < 2:
+            send_box(h, num, j, ring(h, 2, which))
+        else:
+            send(h, num, j, ring(h, 2, which))
+
+    def f2_recv(h, piece):
+        for side in (0, 1):
+            recv(h, F2 + 2 * piece + side, 1 if piece < 2 else 2)
+
+    def px_send(h, piece, drow, which):
+        send_box(h, PX + 6 * piece + 2 * (drow - 1) + which, spot(h, drow, piece, which), partner)
+
+    def px_recv(h, piece, drow):
+        for which in (0, 1):
+            recv(h, PX + 6 * piece + 2 * (drow - 1) + which, 1)
 
     def encode(j0):
         rows = S[pl.ds(2 * j0, 4)].reshape(256, SZ)
@@ -133,27 +171,35 @@
             turned = jnp.where(lane < 32, -pltpu.roll(u, 96, 1), pltpu.roll(u, 32, 1))
             W[pl.ds(pl.multiple_of(8 * j0 + 8 * half, 8), 8), :] = t + turned
 
-    def sib_send(h, drow, piece):
+    def pair(h, c_, drow, piece):
         a, b = pos(h)
-        j0 = sub(h, c, wrap(b + OFFS[drow]), wrap(a + OFFS[piece]), 0)
-        send(h, SIB + 4 * drow + piece, j0, sib, n=2)
-        encode(j0)
-
-    def p1_recv(h, which, side):
-        recv(h, P1 + 2 * which + side)
+        return sub(h, c_, wrap(b + OFFS[drow]), wrap(a + OFFS[piece]), 0)
+
+    earlier = []
+
+    def finish(pairs):
+        for h, drow, piece in pairs:
+            send(h, SIB + 4 * drow + piece, pair(h, c, drow, piece), sib, n=2)
+        for h, drow, piece in pairs:
+            encode(pair(h, c, drow, piece))
+        for h, drow, piece in earlier:
+            recv(h, SIB + 4 * drow + piece, 4)
+        for h, drow, piece in earlier:
+            encode(pair(h, 1 - c, drow, piece))
+        earlier[:] = pairs
 
     local = []
     for h in (0, 1):
-        a, b = pos(h)
-        own = sub(h, c, b, a, zh)
+        own = spot(h, 0, 0, 0)
         src = src_ref.at[pl.ds(2 * h, 2)]
-        send(h, ZX, own, zpart, src=src)
         for side in (0, 1):
             send(h, P1 + side, own, ring(h, 1, side), src=src)
-        p2_send(h, 0, 0, src=src)
+        send(h, ZX, own, zpart, src=src)
         cp = pltpu.make_async_copy(src, at(own), lsem.at[h])
         cp.start()
         local.append(cp)
+    for h in (0, 1):
+        p2_send(h, 0, 0, src=src_ref.at[pl.ds(2 * h + zl, 1)])
 
     S[pl.ds(256, 2)] = jnp.zeros((2, 64, SZ), BF)
     cell = cell_ref[...]
@@ -170,8 +216,8 @@
     QO[...] = dot_nt(hot(4 * (row1 % 64) + row1 // 64 == col), hot(row == cell)).astype(BF)
 
     in_copies[0].wait()
-    pair = ENC2[...].astype(F32)
-    E16[...] = jnp.where(lax.rem(bi, 2) == 1, pair[:, 8:16], pair[:, 0:8]).reshape(16, SZ).astype(BF)
+    two_rows = ENC2[...].astype(F32)
+    E16[...] = jnp.where(lax.rem(bi, 2) == 1, two_rows[:, 8:16], two_rows[:, 0:8]).reshape(16, SZ).astype(BF)
 
     in_copies[1].wait()
     d_i = lax.broadcasted_iota(jnp.int32, (256, 128), 0) % 16
@@ -222,109 +268,106 @@
     def step_t(k):
         lax.fori_loop(k, k + 1, lambda n, _: (build_t(n), 0)[1], 0)
 
+    def step_t(k):
+        lax.fori_loop(k, k + 1, lambda n, _: (build_t(n), 0)[1], 0)
+
+    for cp in local:
+        cp.wait()
+    both = (0, 1)
+
+    for h in both:
+        for side in both:
+            recv(h, P1 + side)
+        send(h, F1, spot(h, 0, 1, 0), ring(h, 1, 0))
+        p2_send(h, 1, 0)
+        p2_send(h, 2, 0)
+    for h in both:
+        recv(h, ZX)
+        for side in both:
+            send(h, P1 + 2 + side, spot(h, 0, 0, 1), ring(h, 1, side))
+        p2_send(h, 0, 1)
+    for h in both:
+        p2_recv(h, 0, 0)
+        f2_send(h, 0, 0)
+        px_send(h, 0, 1, 0)
+        px_send(h, 0, 2, 0)
+    finish([(h, 0, 0) for h in both])
+    step_t(0)
+    for h in both:
+        for side in both:
+            recv(h, P1 + 2 + side)
+        send(h, F1 + 1, spot(h, 0, 2, 1), ring(h, 1, 1))
+        p2_send(h, 1, 1)
+        p2_send(h, 2, 1)
+    finish([(h, 0, piece) for piece in (1, 2) for h in both])
+    for h in both:
+        p2_recv(h, 0, 1)
+        f2_send(h, 0, 1)
+        px_send(h, 0, 1, 1)
+        px_send(h, 0, 2, 1)
+    step_t(1)
+    for h in both:
+        for side in both:
+            recv(h, F1 + side)
+        p2_send(h, 3, 0)
+        p2_send(h, 3, 1)
+    finish([(h, 0, 3) for h in both])
+    step_t(2)
+    for h in both:
+        p2_recv(h, 1, 0)
+        f2_send(h, 1, 0)
+        px_send(h, 1, 1, 0)
+        px_send(h, 1, 2, 0)
+    for h in both:
+        for drow in (1, 2):
+            px_recv(h, 0, drow)
+    finish([(h, drow, 0) for drow in (1, 2) for h in both])
+    step_t(3)
+    for h in both:
+        p2_recv(h, 1, 1)
+        f2_send(h, 1, 1)
+        px_send(h, 1, 1, 1)
+        px_send(h, 1, 2, 1)
+    for h in both:
+        f2_recv(h, 0)
+        px_send(h, 0, 3, 0)
+        px_send(h, 0, 3, 1)
+    step_t(4)
+    for h in both:
+        for which in both:
+            p2_recv(h, 2, which)
+            f2_send(h, 2, which)
+    finish([(h, drow, 2) for drow in (1, 2) for h in both])
+    step_t(5)
+    for h in both:
+        f2_recv(h, 1)
+        px_send(h, 1, 3, 0)
+        px_send(h, 1, 3, 1)
+    for h in both:
+        for drow in (1, 2):
+            px_recv(h, 1, drow)
+        px_recv(h, 0, 3)
+    finish([(h, drow, 1) for drow in (1, 2) for h in both] + [(h, 3, 0) for h in both])
+    step_t(6)
+    for h in both:
+        for which in both:
+            p2_recv(h, 3, which)
+            f2_send(h, 3, which)
+    finish([(h, drow, 3) for drow in (1, 2) for h in both])
+    step_t(7)
     in_copies[2].wait()
     build_d(False)
     build_d(True)
-    for cp in local:
-        cp.wait()
-
-    step_t(0)
-
-    for h in (0, 1):
-        a, b = pos(h)
-        recv(h, ZX)
-        other = sub(h, c, b, a, 1 - zh)
-        for side in (0, 1):
-            send(h, P1 + 2 + side, other, ring(h, 1, side))
-        p2_send(h, 0, 1)
-        sib_send(h, 0, 0)
-
-    for h in (0, 1):
-        a, b = pos(h)
-        for side in (0, 1):
-            p1_recv(h, 0, side)
-        send(h, F1, sub(h, c, b, wrap(a - 1), zh), ring(h, 1, 0))
-        p2_send(h, 1, 0)
-        p2_send(h, 2, 0)
-
-    step_t(1)
-
-    for h in (0, 1):
-        a, b = pos(h)
-        for side in (0, 1):
-            recv(h, P2 + side)
-        send(h, F2, sub(h, c, wrap(b - 1), a, zh), ring(h, 2, 0))
-
-    step_t(2)
-
-    for h in (0, 1):
-        a, b = pos(h)
-        for side in (0, 1):
-            p1_recv(h, 1, side)
-        send(h, F1 + 1, sub(h, c, b, wrap(a + 1), 1 - zh), ring(h, 1, 1))
-        p2_send(h, 1, 1)
-        p2_send(h, 2, 1)
-        sib_send(h, 0, 1)
-        sib_send(h, 0, 2)
-
-    step_t(3)
-
-    for h in (0, 1):
-        a, b = pos(h)
-        for side in (0, 1):
-            recv(h, P2 + 2 + side)
-        send(h, F2 + 1, sub(h, c, wrap(b + 1), a, 1 - zh), ring(h, 2, 1))
-        sib_send(h, 1, 0)
-        sib_send(h, 2, 0)
-
-    step_t(4)
-
-    for h in (0, 1):
-        for side in (0, 1):
-            recv(h, F1 + side)
-        p2_send(h, 3, 0)
-        p2_send(h, 3, 1)
-        sib_send(h, 0, 3)
-
-    step_t(5)
-
-    def relay(h, piece):
-        a, b = pos(h)
-        p1 = wrap(a + OFFS[piece])
-        for which in (0, 1):
-            for side in (0, 1):
-                recv(h, P2 + 4 * piece + 2 * which + side)
-            if which == 0:
-                send(h, F2 + 2 * piece, sub(h, c, wrap(b - 1), p1, zh), ring(h, 2, 0))
-            else:
-                send(h, F2 + 2 * piece + 1, sub(h, c, wrap(b + 1), p1, 1 - zh), ring(h, 2, 1))
-        sib_send(h, 1, piece)
-        sib_send(h, 2, piece)
-
-    for piece in (1, 2):
-        for h in (0, 1):
-            relay(h, piece)
-        step_t(5 + piece)
-    for h in (0, 1):
-        relay(h, 3)
-
-    for piece in range(4):
-        for h in (0, 1):
-            for side in (0, 1):
-                recv(h, F2 + 2 * piece + side)
-            sib_send(h, 3, piece)
-
-    for drow in range(4):
-        for piece in range(4):
-            for h in (0, 1):
-                a, b = pos(h)
-                recv(h, SIB + 4 * drow + piece, n=2)
-                encode(sub(h, 1 - c, wrap(b + OFFS[drow]), wrap(a + OFFS[piece]), 0))
+    for h in both:
+        f2_recv(h, 2)
+        px_recv(h, 1, 3)
+    finish([(h, 3, piece) for piece in (1, 2) for h in both])
+    for h in both:
+        f2_recv(h, 3)
+    finish([(h, 3, 3) for h in both])
+    finish([])
 
     pl.semaphore_signal(ready, inc=1, device_id=partner, device_id_type=MESH)
-    for cp in started:
-        cp.wait_send()
-
     lane64 = lax.broadcasted_iota(jnp.int32, (256, 64), 1)
     quarter = lax.broadcasted_iota(jnp.int32, (64, 128), 1) // 32
 
@@ -336,8 +379,8 @@
         t_hi = TT[k, 0].reshape(512, 256)
         t_lo = TT[k, 1].reshape(512, 256)
         nn = (((1,), (0,)), ((), ()))
-        f = lax.dot_general(t_hi, hi, nn, preferred_element_type=F32)
-        f = f + lax.dot_general(t_hi, lo, nn, preferred_element_type=F32)
+        wide = lax.dot_general(t_hi, jnp.concatenate([hi, lo], axis=1), nn, preferred_element_type=F32)
+        f = wide[:, 0:64] + wide[:, 64:128]
         f = f + lax.dot_general(t_lo, hi, nn, preferred_element_type=F32)
         fr, fi = f[0:256], f[256:512]
         swapped = jnp.concatenate([fi[:, 32:64], fi[:, 0:32]], axis=1)
@@ -353,7 +396,7 @@
             V[pl.ds(8 * ri + k, 64, stride=16), :] = val
         return 0
 
-    lax.fori_loop(0, KD, translate, 0)
+    lax.fori_loop(0, KD, translate, 0, unroll=2)
     SEND[...] = V[...].astype(BF).reshape(64, 16, 128)
     R[pl.ds(bi, 1)] = SEND[pl.ds(bi, 1)]
 
@@ -410,6 +453,8 @@
                               + NEAR[q, ro, :, pl.ds(mine, 128)] + NR[q, ro])
     sent = SEND.at[pl.ds(0, NB - 1)]
     pltpu.make_async_copy(sent, sent, a2s.at[0]).wait()
+    for cp in started:
+        cp.wait_send()
     far_out.wait()
     for q in range(4):
         for ro in range(2):

time: 62.1 us -> 62.7 us (level)
  no operation moved by 1% of the time
where the time goes in v2:
time: 62.7 us; the launch traced here: 62.5 us
  Pallas kernels  60.9 us (97%)
  local copies, waits for them, and re-layouts  1.57 us (3%)
    pallas_call x1, Pallas kernels, on_device(): pl.pallas_call(body, out_shape=jax.ShapeDtypeStruct((PER, 2, RHS, 128), F...  60.9 us
    unnamed x1, local copies, waits for them, and re-layouts  1.57 us

profile of v2, /device:TPU:1, one launch (start us, length us, event | category | flops | bytes accessed | tf_op | source)
XLA Modules:
  0.0 62.5 jit_solution(10186136771948174367)
XLA Ops:
  0.0 60.9 %fmm.1 = f32[4,2,32,128]{3,2,1,0:T(8,128)} custom-call(s32[4,14]{1,0:T(4,128)} %list_ref.1, s32[4,14]{1,0:T(4,128)} %mask_ref.1, s32[1,256]{1,0:T(1,128)} %bitcast.5, bf16[4,64,256]{2,1,0:T(8,128)(2,1)} %bitcast.4, bf16[2,512,256]{2,1,0:T(8,128)(2,1)} %enc_hbm.1, f32[8,2,16,128]{3,2,1,0:T(8,128)} %ker_hbm.1, bf16[2,512,256]{2,1,0:T(8,128)(2,1)} %dec_hbm.1, ...), custom_call_target="tpu_custom_call" | custom-call | tf_op jit(solution)/shard_map/fmm/pallas_call | solution.py:469
  61.0 1.6 %copy.10 = f32[4,2,32,128]{3,2,1,0:T(8,128)} copy(f32[4,2,32,128]{3,2,1,0:T(8,128)} %fmm.1) | data formatting | bytes 262144

commit v3 on v2

--- a/solution.py
+++ b/solution.py
@@ -154,7 +154,8 @@
             recv(h, F2 + 2 * piece + side, 1 if piece < 2 else 2)
 
     def px_send(h, piece, drow, which):
-        send_box(h, PX + 6 * piece + 2 * (drow - 1) + which, spot(h, drow, piece, which), partner)
+        send_box(h, PX + 6 * piece + 2 * (drow - 1) + which, spot(h, drow, piece, which),
+                 partner if piece == 0 else zpart)
 
     def px_recv(h, piece, drow):
         for which in (0, 1):
@@ -300,11 +301,22 @@
         p2_send(h, 1, 1)
         p2_send(h, 2, 1)
     finish([(h, 0, piece) for piece in (1, 2) for h in both])
-    for h in both:
-        p2_recv(h, 0, 1)
-        f2_send(h, 0, 1)
-        px_send(h, 0, 1, 1)
-        px_send(h, 0, 2, 1)
+
+    def p2_relay(h, piece, which):
+        p2_recv(h, piece, which)
+        f2_send(h, piece, which)
+        if piece < 2:
+            px_send(h, piece, 1, which)
+            px_send(h, piece, 2, which)
+
+    def f2_relay(h, piece):
+        f2_recv(h, piece)
+        px_send(h, piece, 3, 0)
+        px_send(h, piece, 3, 1)
+
+    for h in both:
+        p2_relay(h, 0, 1)
+        p2_relay(h, 1, 0)
     step_t(1)
     for h in both:
         for side in both:
@@ -314,54 +326,41 @@
     finish([(h, 0, 3) for h in both])
     step_t(2)
     for h in both:
-        p2_recv(h, 1, 0)
-        f2_send(h, 1, 0)
-        px_send(h, 1, 1, 0)
-        px_send(h, 1, 2, 0)
+        f2_relay(h, 0)
+        p2_relay(h, 1, 1)
+    step_t(3)
+    for h in both:
+        p2_relay(h, 2, 0)
+        p2_relay(h, 2, 1)
+    finish([(h, drow, 2) for drow in (1, 2) for h in both])
+    step_t(4)
+    for h in both:
+        f2_relay(h, 1)
     for h in both:
         for drow in (1, 2):
             px_recv(h, 0, drow)
     finish([(h, drow, 0) for drow in (1, 2) for h in both])
-    step_t(3)
-    for h in both:
-        p2_recv(h, 1, 1)
-        f2_send(h, 1, 1)
-        px_send(h, 1, 1, 1)
-        px_send(h, 1, 2, 1)
-    for h in both:
-        f2_recv(h, 0)
-        px_send(h, 0, 3, 0)
-        px_send(h, 0, 3, 1)
-    step_t(4)
-    for h in both:
-        for which in both:
-            p2_recv(h, 2, which)
-            f2_send(h, 2, which)
-    finish([(h, drow, 2) for drow in (1, 2) for h in both])
     step_t(5)
     for h in both:
-        f2_recv(h, 1)
-        px_send(h, 1, 3, 0)
-        px_send(h, 1, 3, 1)
+        p2_relay(h, 3, 0)
+        p2_relay(h, 3, 1)
+    finish([(h, drow, 3) for drow in (1, 2) for h in both])
+    step_t(6)
     for h in both:
         for drow in (1, 2):
             px_recv(h, 1, drow)
-        px_recv(h, 0, 3)
-    finish([(h, drow, 1) for drow in (1, 2) for h in both] + [(h, 3, 0) for h in both])
-    step_t(6)
-    for h in both:
-        for which in both:
-            p2_recv(h, 3, which)
-            f2_send(h, 3, which)
-    finish([(h, drow, 3) for drow in (1, 2) for h in both])
+    finish([(h, drow, 1) for drow in (1, 2) for h in both])
     step_t(7)
     in_copies[2].wait()
     build_d(False)
     build_d(True)
     for h in both:
+        px_recv(h, 0, 3)
         f2_recv(h, 2)
+    finish([(h, 3, piece) for piece in (0, 2) for h in both])
+    for h in both:
         px_recv(h, 1, 3)
-    finish([(h, 3, piece) for piece in (1, 2) for h in both])
+    finish([(h, 3, 1) for h in both])
     for h in both:
         f2_recv(h, 3)
     finish([(h, 3, 3) for h in both])

time: 62.7 us -> 56.6 us (0.903)
  Pallas kernels: 60.9 us -> 54.8 us
    pallas_call x1, Pallas kernels: 60.9 us -> 54.8 us  [on_device(): pl.pallas_call(body, out_shape=jax.ShapeDtypeStruct((PER, 2, RHS, 128), F...]
where the time goes in v3:
time: 56.6 us; the launch traced here: 56.4 us
  Pallas kernels  54.8 us (97%)
  local copies, waits for them, and re-layouts  1.57 us (3%)
    pallas_call x1, Pallas kernels, on_device(): pl.pallas_call(body, out_shape=jax.ShapeDtypeStruct((PER, 2, RHS, 128), F...  54.8 us
    unnamed x1, local copies, waits for them, and re-layouts  1.57 us

profile of v3, /device:TPU:1, one launch (start us, length us, event | category | flops | bytes accessed | tf_op | source)
XLA Modules:
  0.0 56.4 jit_solution(450757811667608549)
XLA Ops:
  0.0 54.8 %fmm.1 = f32[4,2,32,128]{3,2,1,0:T(8,128)} custom-call(s32[4,14]{1,0:T(4,128)} %list_ref.1, s32[4,14]{1,0:T(4,128)} %mask_ref.1, s32[1,256]{1,0:T(1,128)} %bitcast.5, bf16[4,64,256]{2,1,0:T(8,128)(2,1)} %bitcast.4, bf16[2,512,256]{2,1,0:T(8,128)(2,1)} %enc_hbm.1, f32[8,2,16,128]{3,2,1,0:T(8,128)} %ker_hbm.1, bf16[2,512,256]{2,1,0:T(8,128)(2,1)} %dec_hbm.1, ...), custom_call_target="tpu_custom_call" | custom-call | tf_op jit(solution)/shard_map/fmm/pallas_call | solution.py:468
  54.8 1.6 %copy.10 = f32[4,2,32,128]{3,2,1,0:T(8,128)} copy(f32[4,2,32,128]{3,2,1,0:T(8,128)} %fmm.1) | data formatting | bytes 262144

commit v4 on v3

--- a/solution.py
+++ b/solution.py
@@ -110,8 +110,19 @@
             src_ref=src, dst_ref=dst,
             send_sem=ssem.at[h * HALF + num], recv_sem=rsem.at[h * HALF + num],
             device_id=device, device_id_type=MESH)
-        cp.start()
         started.append(cp)
+        held[h].append(cp)
+
+    held = ([], [])
+
+    def flush():
+        a, b = held
+        for n in range(max(len(a), len(b))):
+            for side in (a, b):
+                if n < len(side):
+                    side[n].start()
+        a.clear()
+        b.clear()
 
     def send(h, num, j, device, n=1, src=None):
         copy(h, num, at(j, n) if src is None else src, at(j, n), device)
@@ -179,8 +190,10 @@
     earlier = []
 
     def finish(pairs):
+        flush()
         for h, drow, piece in pairs:
             send(h, SIB + 4 * drow + piece, pair(h, c, drow, piece), sib, n=2)
+        flush()
         for h, drow, piece in pairs:
             encode(pair(h, c, drow, piece))
         for h, drow, piece in earlier:
@@ -201,6 +214,7 @@
         local.append(cp)
     for h in (0, 1):
         p2_send(h, 0, 0, src=src_ref.at[pl.ds(2 * h + zl, 1)])
+    flush()
 
     S[pl.ds(256, 2)] = jnp.zeros((2, 64, SZ), BF)
     cell = cell_ref[...]
@@ -267,89 +281,96 @@
                 TT[k, part, ri] = dot_nt(first, QI[...]).astype(BF)
 
     def step_t(k):
+        flush()
         lax.fori_loop(k, k + 1, lambda n, _: (build_t(n), 0)[1], 0)
 
     def step_t(k):
+        flush()
         lax.fori_loop(k, k + 1, lambda n, _: (build_t(n), 0)[1], 0)
 
     for cp in local:
         cp.wait()
     both = (0, 1)
 
-    for h in both:
-        for side in both:
-            recv(h, P1 + side)
-        send(h, F1, spot(h, 0, 1, 0), ring(h, 1, 0))
-        p2_send(h, 1, 0)
-        p2_send(h, 2, 0)
-    for h in both:
-        recv(h, ZX)
-        for side in both:
-            send(h, P1 + 2 + side, spot(h, 0, 0, 1), ring(h, 1, side))
-        p2_send(h, 0, 1)
-    for h in both:
-        p2_recv(h, 0, 0)
-        f2_send(h, 0, 0)
-        px_send(h, 0, 1, 0)
-        px_send(h, 0, 2, 0)
-    finish([(h, 0, 0) for h in both])
-    step_t(0)
-    for h in both:
-        for side in both:
-            recv(h, P1 + 2 + side)
-        send(h, F1 + 1, spot(h, 0, 2, 1), ring(h, 1, 1))
-        p2_send(h, 1, 1)
-        p2_send(h, 2, 1)
-    finish([(h, 0, piece) for piece in (1, 2) for h in both])
-
     def p2_relay(h, piece, which):
         p2_recv(h, piece, which)
-        f2_send(h, piece, which)
         if piece < 2:
             px_send(h, piece, 1, which)
             px_send(h, piece, 2, which)
+        f2_send(h, piece, which)
 
     def f2_relay(h, piece):
         f2_recv(h, piece)
         px_send(h, piece, 3, 0)
         px_send(h, piece, 3, 1)
 
-    for h in both:
-        p2_relay(h, 0, 1)
-        p2_relay(h, 1, 0)
+    def relay(*steps):
+        for piece, which in steps:
+            for h in both:
+                p2_relay(h, piece, which)
+            flush()
+
+    for h in both:
+        for side in both:
+            recv(h, P1 + side)
+        send(h, F1, spot(h, 0, 1, 0), ring(h, 1, 0))
+    flush()
+    for h in both:
+        recv(h, ZX)
+        for side in both:
+            send(h, P1 + 2 + side, spot(h, 0, 0, 1), ring(h, 1, side))
+    flush()
+    for h in both:
+        p2_send(h, 1, 0)
+        p2_send(h, 0, 1)
+        p2_send(h, 2, 0)
+    flush()
+    relay((0, 0))
+    finish([(h, 0, 0) for h in both])
+    step_t(0)
+    for h in both:
+        for side in both:
+            recv(h, P1 + 2 + side)
+        send(h, F1 + 1, spot(h, 0, 2, 1), ring(h, 1, 1))
+    flush()
+    for h in both:
+        recv(h, F1)
+        p2_send(h, 3, 0)
+    flush()
+    for h in both:
+        p2_send(h, 1, 1)
+        p2_send(h, 2, 1)
+    finish([(h, 0, piece) for piece in (1, 2) for h in both])
+    relay((0, 1), (1, 0))
     step_t(1)
     for h in both:
-        for side in both:
-            recv(h, F1 + side)
-        p2_send(h, 3, 0)
+        recv(h, F1 + 1)
         p2_send(h, 3, 1)
     finish([(h, 0, 3) for h in both])
     step_t(2)
     for h in both:
         f2_relay(h, 0)
-        p2_relay(h, 1, 1)
+    flush()
+    relay((2, 0), (1, 1))
     step_t(3)
-    for h in both:
-        p2_relay(h, 2, 0)
-        p2_relay(h, 2, 1)
+    relay((3, 0), (2, 1))
     finish([(h, drow, 2) for drow in (1, 2) for h in both])
     step_t(4)
     for h in both:
         f2_relay(h, 1)
+    flush()
+    relay((3, 1))
+    finish([(h, drow, 3) for drow in (1, 2) for h in both])
     for h in both:
         for drow in (1, 2):
             px_recv(h, 0, drow)
     finish([(h, drow, 0) for drow in (1, 2) for h in both])
     step_t(5)
     for h in both:
-        p2_relay(h, 3, 0)
-        p2_relay(h, 3, 1)
-    finish([(h, drow, 3) for drow in (1, 2) for h in both])
-    step_t(6)
-    for h in both:
         for drow in (1, 2):
             px_recv(h, 1, drow)
     finish([(h, drow, 1) for drow in (1, 2) for h in both])
+    step_t(6)
     step_t(7)
     in_copies[2].wait()
     build_d(False)
@@ -395,7 +416,7 @@
             V[pl.ds(8 * ri + k, 64, stride=16), :] = val
         return 0
 
-    lax.fori_loop(0, KD, translate, 0, unroll=2)
+    lax.fori_loop(0, KD, translate, 0, unroll=4)
     SEND[...] = V[...].astype(BF).reshape(64, 16, 128)
     R[pl.ds(bi, 1)] = SEND[pl.ds(bi, 1)]
 

time: 56.6 us -> 54.3 us (0.959)
  Pallas kernels: 54.8 us -> 52.6 us
    pallas_call x1, Pallas kernels: 54.8 us -> 52.6 us  [on_device(): pl.pallas_call(body, out_shape=jax.ShapeDtypeStruct((PER, 2, RHS, 128), F...]
where the time goes in v4:
time: 54.3 us; the launch traced here: 54.1 us
  Pallas kernels  52.6 us (97%)
  local copies, waits for them, and re-layouts  1.57 us (3%)
    pallas_call x1, Pallas kernels, on_device(): pl.pallas_call(body, out_shape=jax.ShapeDtypeStruct((PER, 2, RHS, 128), F...  52.6 us
    unnamed x1, local copies, waits for them, and re-layouts  1.57 us

profile of v4, /device:TPU:1, one launch (start us, length us, event | category | flops | bytes accessed | tf_op | source)
XLA Modules:
  0.0 54.1 jit_solution(7731700458004887063)
XLA Ops:
  0.0 52.6 %fmm.1 = f32[4,2,32,128]{3,2,1,0:T(8,128)} custom-call(s32[4,14]{1,0:T(4,128)} %list_ref.1, s32[4,14]{1,0:T(4,128)} %mask_ref.1, s32[1,256]{1,0:T(1,128)} %bitcast.5, bf16[4,64,256]{2,1,0:T(8,128)(2,1)} %bitcast.4, bf16[2,512,256]{2,1,0:T(8,128)(2,1)} %enc_hbm.1, f32[8,2,16,128]{3,2,1,0:T(8,128)} %ker_hbm.1, bf16[2,512,256]{2,1,0:T(8,128)(2,1)} %dec_hbm.1, ...), custom_call_target="tpu_custom_call" | custom-call | tf_op jit(solution)/shard_map/fmm/pallas_call | solution.py:489
  52.6 1.6 %copy.10 = f32[4,2,32,128]{3,2,1,0:T(8,128)} copy(f32[4,2,32,128]{3,2,1,0:T(8,128)} %fmm.1) | data formatting | bytes 262144

commit v5 on v4

--- a/solution.py
+++ b/solution.py
@@ -328,6 +328,7 @@
     relay((0, 0))
     finish([(h, 0, 0) for h in both])
     step_t(0)
+    step_t(1)
     for h in both:
         for side in both:
             recv(h, P1 + 2 + side)
@@ -342,20 +343,25 @@
         p2_send(h, 2, 1)
     finish([(h, 0, piece) for piece in (1, 2) for h in both])
     relay((0, 1), (1, 0))
-    step_t(1)
+    step_t(2)
+    step_t(3)
     for h in both:
         recv(h, F1 + 1)
         p2_send(h, 3, 1)
     finish([(h, 0, 3) for h in both])
-    step_t(2)
+    step_t(4)
+    step_t(5)
+    in_copies[2].wait()
+    build_d(False)
+    build_d(True)
     for h in both:
         f2_relay(h, 0)
     flush()
     relay((2, 0), (1, 1))
-    step_t(3)
+    step_t(6)
     relay((3, 0), (2, 1))
     finish([(h, drow, 2) for drow in (1, 2) for h in both])
-    step_t(4)
+    step_t(7)
     for h in both:
         f2_relay(h, 1)
     flush()
@@ -365,16 +371,13 @@
         for drow in (1, 2):
             px_recv(h, 0, drow)
     finish([(h, drow, 0) for drow in (1, 2) for h in both])
-    step_t(5)
+    flush()
     for h in both:
         for drow in (1, 2):
             px_recv(h, 1, drow)
     finish([(h, drow, 1) for drow in (1, 2) for h in both])
-    step_t(6)
-    step_t(7)
-    in_copies[2].wait()
-    build_d(False)
-    build_d(True)
+    flush()
+    flush()
     for h in both:
         px_recv(h, 0, 3)
         f2_recv(h, 2)

time: 54.3 us -> 53.1 us (0.978)
  Pallas kernels: 52.6 us -> 51.4 us
    pallas_call x1, Pallas kernels: 52.6 us -> 51.4 us  [on_device(): pl.pallas_call(body, out_shape=jax.ShapeDtypeStruct((PER, 2, RHS, 128), F...]
where the time goes in v5:
time: 53.1 us; the launch traced here: 52.9 us
  Pallas kernels  51.4 us (97%)
  local copies, waits for them, and re-layouts  1.57 us (3%)
    pallas_call x1, Pallas kernels, on_device(): pl.pallas_call(body, out_shape=jax.ShapeDtypeStruct((PER, 2, RHS, 128), F...  51.4 us
    unnamed x1, local copies, waits for them, and re-layouts  1.57 us

profile of v5, /device:TPU:1, one launch (start us, length us, event | category | flops | bytes accessed | tf_op | source)
XLA Modules:
  0.0 52.9 jit_solution(8078234555808071289)
XLA Ops:
  0.0 51.4 %fmm.1 = f32[4,2,32,128]{3,2,1,0:T(8,128)} custom-call(s32[4,14]{1,0:T(4,128)} %list_ref.1, s32[4,14]{1,0:T(4,128)} %mask_ref.1, s32[1,256]{1,0:T(1,128)} %bitcast.5, bf16[4,64,256]{2,1,0:T(8,128)(2,1)} %bitcast.4, bf16[2,512,256]{2,1,0:T(8,128)(2,1)} %enc_hbm.1, f32[8,2,16,128]{3,2,1,0:T(8,128)} %ker_hbm.1, bf16[2,512,256]{2,1,0:T(8,128)(2,1)} %dec_hbm.1, ...), custom_call_target="tpu_custom_call" | custom-call | tf_op jit(solution)/shard_map/fmm/pallas_call | solution.py:492
  51.4 1.6 %copy.10 = f32[4,2,32,128]{3,2,1,0:T(8,128)} copy(f32[4,2,32,128]{3,2,1,0:T(8,128)} %fmm.1) | data formatting | bytes 262144

commit v6 on v5

--- a/solution.py
+++ b/solution.py
@@ -48,7 +48,7 @@
 
 
 def body(list_ref, mask_ref, cell_ref, src_ref, enc_hbm, ker_hbm, dec_hbm, nb_hbm, out_ref,
-         S, W, TT, D, V, SEND, R, NBV, NEAR, NS, NR, FS, FR, QI, QO, BASE, ENC2, E16, KER, DEC,
+         S, W, TT, D, V, SEND, R, NBV, NEAR, FS, FR, QI, QO, BASE, ENC2, E16, KER, DEC,
          ssem, rsem, lsem, nsem, isem, a2s, a2r, pss, psr, ready):
     bi = lax.axis_index("box")
     zl = lax.axis_index("dir")
@@ -450,34 +450,33 @@
 
     mine = pl.multiple_of(128 * zl, 128)
     theirs = pl.multiple_of(128 * (1 - zl), 128)
-    NS[...] = NEAR[:, :, :, pl.ds(theirs, 128)]
-    near_out = pltpu.make_async_remote_copy(
-        src_ref=NS, dst_ref=NR, send_sem=pss.at[0], recv_sem=psr.at[0],
-        device_id=partner, device_id_type=MESH)
-    near_out.start()
-
+
+    for cp in started:
+        cp.wait_send()
     whole = R.at[pl.ds(0, NB - 1)]
+    sent = SEND.at[pl.ds(0, NB - 1)]
+    pltpu.make_async_copy(sent, sent, a2s.at[0]).wait()
     pltpu.make_async_copy(whole, whole, a2r.at[0]).wait()
     got = R[...].reshape(1024, 128)
 
     def decode(which):
         return lax.dot_general(got, D[which], (((0,), (0,)), ((), ())), preferred_element_type=F32)
 
-    FS[...] = decode(1).astype(BF)
+    far = decode(1)
+    for q in range(4):
+        for ro in range(2):
+            FS[32 * q:32 * q + 32, 128 * ro:128 * ro + 128] = (
+                far[32 * q:32 * q + 32, 128 * ro:128 * ro + 128]
+                + NEAR[q, ro, :, pl.ds(theirs, 128)]).astype(BF)
     far_out = pltpu.make_async_remote_copy(
-        src_ref=FS, dst_ref=FR, send_sem=pss.at[1], recv_sem=psr.at[1],
+        src_ref=FS, dst_ref=FR, send_sem=pss.at[0], recv_sem=psr.at[0],
         device_id=partner, device_id_type=MESH)
     far_out.start()
     far = decode(0)
-    near_out.wait()
     for q in range(4):
         for ro in range(2):
             out_ref[q, ro] = (far[32 * q:32 * q + 32, 128 * ro:128 * ro + 128]
-                              + NEAR[q, ro, :, pl.ds(mine, 128)] + NR[q, ro])
-    sent = SEND.at[pl.ds(0, NB - 1)]
-    pltpu.make_async_copy(sent, sent, a2s.at[0]).wait()
-    for cp in started:
-        cp.wait_send()
+                              + NEAR[q, ro, :, pl.ds(mine, 128)])
     far_out.wait()
     for q in range(4):
         for ro in range(2):
@@ -504,8 +503,6 @@
             pltpu.VMEM((NB, 16, 128), BF),
             pltpu.VMEM((PER, SLOTS, 512, SZ), BF),
             pltpu.VMEM((PER, 2, RHS, SZ), F32),
-            pltpu.VMEM((PER, 2, RHS, 128), F32),
-            pltpu.VMEM((PER, 2, RHS, 128), F32),
             pltpu.VMEM((128, 256), BF),
             pltpu.VMEM((128, 256), BF),
             pltpu.VMEM((256, 256), BF),
@@ -522,8 +519,8 @@
             pltpu.SemaphoreType.DMA((3,)),
             pltpu.SemaphoreType.DMA((1,)),
             pltpu.SemaphoreType.DMA((1,)),
-            pltpu.SemaphoreType.DMA((2,)),
-            pltpu.SemaphoreType.DMA((2,)),
+            pltpu.SemaphoreType.DMA((1,)),
+            pltpu.SemaphoreType.DMA((1,)),
             pltpu.SemaphoreType.REGULAR,
         ],
         compiler_params=pltpu.CompilerParams(

time: 53.1 us -> 53 us (level)
  no operation moved by 1% of the time
where the time goes in v6:
time: 53 us; the launch traced here: 52.8 us
  Pallas kernels  51.3 us (97%)
  local copies, waits for them, and re-layouts  1.57 us (3%)
    pallas_call x1, Pallas kernels, on_device(): pl.pallas_call(body, out_shape=jax.ShapeDtypeStruct((PER, 2, RHS, 128), F...  51.3 us
    unnamed x1, local copies, waits for them, and re-layouts  1.57 us

profile of v6, /device:TPU:1, one launch (start us, length us, event | category | flops | bytes accessed | tf_op | source)
XLA Modules:
  0.0 52.8 jit_solution(9381990361308543930)
XLA Ops:
  0.0 51.3 %fmm.1 = f32[4,2,32,128]{3,2,1,0:T(8,128)} custom-call(s32[4,14]{1,0:T(4,128)} %list_ref.1, s32[4,14]{1,0:T(4,128)} %mask_ref.1, s32[1,256]{1,0:T(1,128)} %bitcast.5, bf16[4,64,256]{2,1,0:T(8,128)(2,1)} %bitcast.4, bf16[2,512,256]{2,1,0:T(8,128)(2,1)} %enc_hbm.1, f32[8,2,16,128]{3,2,1,0:T(8,128)} %ker_hbm.1, bf16[2,512,256]{2,1,0:T(8,128)(2,1)} %dec_hbm.1, ...), custom_call_target="tpu_custom_call" | custom-call | tf_op jit(solution)/shard_map/fmm/pallas_call | solution.py:491
  51.3 1.6 %copy.10 = f32[4,2,32,128]{3,2,1,0:T(8,128)} copy(f32[4,2,32,128]{3,2,1,0:T(8,128)} %fmm.1) | data formatting | bytes 262144
